TPU v7x, 32 devices: a whole 2x2x4 slice. The times are simulated.
32 devices in a mesh: ctx: 4 (over y, x), dp: 8 (over z, core).
Axes of the slice: x: 2, y: 2, z: 4, core: 2. Of those that a mesh axis runs over, the one named last changes fastest.
Arguments:
- queries: bfloat16 [8, 512, 1024], P('dp', 'ctx'), may hold values from -6 to 6
- keys_in: bfloat16 [8, 512, 256], P('dp', 'ctx'), may hold values from -6 to 6
- values_in: bfloat16 [8, 512, 256], P('dp', 'ctx'), may hold values from -6 to 6
- patch_order: int32 [8, 4, 128], P('dp', 'ctx'), may hold values from 0 to 127, each once within a row
- block_mask: int32 [8, 16, 8], P('dp', 'ctx'), may hold values 0 or 1
- out_weight: bfloat16 [1024, 1024], P('dp'), may hold values from -0.1875 to 0.1875
- cotangent: bfloat16 [8, 512, 1024], P('dp', 'ctx'), may hold values from -6 to 6
Outputs:
- mixed: bfloat16 [8, 512, 1024], P('dp', 'ctx')
- grad_queries: bfloat16 [8, 512, 1024], P('dp', 'ctx')
- grad_keys: bfloat16 [8, 512, 256], P('dp', 'ctx')
- grad_values: bfloat16 [8, 512, 256], P('dp', 'ctx')
- grad_weight: float32 [1024, 1024], P('dp', 'ctx')
Inputs may be any that keep to these rules, and one draw needn't show every extreme that they name: `patch_order`: each row of 128 entries is a permutation.
All inputs are finite; a program needn't handle non-finite values. No bound on the sum of `block_mask` on one device may be relied on, other than what follows from the above.
Results may differ from a plain program's by a relative error of at most 0.015.
Values may be sent and summed in bfloat16 or wider, within the bound.
No kernel may reach another device: no remote copies, remote signals or barrier semaphores. Data moves between devices by JAX's collectives and lax.ppermute only.
A program may use at most 64 MiB of HBM per device.

v0:
```python
import math
import jax
import jax.numpy as jnp
from jax import lax
from jax.sharding import PartitionSpec as P

QUERY_HEADS = 8
KEY_VALUE_HEADS = 2
HEAD_WIDTH = 128
BLK = 32


def with_halo(block, sides, width):
    for axis, dim in sides:
        count = lax.axis_size(axis)
        forward = [(i, i + 1) for i in range(count - 1)]
        forward.append((count - 1, 0))
        backward = [(target, source) for source, target in forward]
        low = lax.ppermute(
            lax.slice_in_dim(block, block.shape[dim] - width, None, axis=dim), axis, forward
        )
        high = lax.ppermute(lax.slice_in_dim(block, 0, width, axis=dim), axis, backward)
        block = jnp.concatenate([low, block, high], axis=dim)
    return block


def shards(queries, keys_in, values_in, patch_order, block_mask, out_weight, cotangent):
    scale = 1.0 / math.sqrt(HEAD_WIDTH)
    query_group = QUERY_HEADS // KEY_VALUE_HEADS
    token_rows = queries.shape[1]
    key_head_width = keys_in.shape[2]
    row_position = patch_order[0, 0]
    query_sequence = jnp.take(queries[0], row_position, axis=0)
    key_sequence = jnp.take(keys_in[0], row_position, axis=0)
    value_sequence = jnp.take(values_in[0], row_position, axis=0)
    dy_seq = jnp.take(cotangent[0], row_position, axis=0)
    kv_pair = jnp.concatenate([key_sequence, value_sequence], axis=1)
    neighbour_band = with_halo(kv_pair, (("ctx", 0),), token_rows)
    key_band = neighbour_band[:, :key_head_width].reshape(
        3 * token_rows, KEY_VALUE_HEADS, HEAD_WIDTH
    )
    value_band = neighbour_band[:, key_head_width:].reshape(
        3 * token_rows, KEY_VALUE_HEADS, HEAD_WIDTH
    )
    weight_all = lax.all_gather(out_weight, "dp", axis=0, tiled=True)
    expanded = jnp.repeat(jnp.repeat(block_mask[0], BLK, 0), BLK, 1) > 0
    allowed = jnp.concatenate(
        [
            expanded[:, :token_rows],
            jnp.ones((token_rows, token_rows), bool),
            expanded[:, token_rows:],
        ],
        1,
    )
    allowed = allowed[None, None]
    query_four = query_sequence.reshape(token_rows, KEY_VALUE_HEADS, query_group, HEAD_WIDTH)
    scores = (
        jnp.einsum("tkgd,skd->kgts", query_four, key_band, preferred_element_type=jnp.float32)
        * scale
    )
    scores = jnp.where(allowed, scores, -1e30)
    highest = jnp.max(scores, axis=-1, keepdims=True)
    weights = jnp.where(allowed, jnp.exp(scores - highest), 0.0)
    probs = weights / jnp.sum(weights, axis=-1, keepdims=True)
    probs_b = probs.astype(jnp.bfloat16)
    attended_f = jnp.einsum(
        "kgts,skd->tkgd", probs_b, value_band, preferred_element_type=jnp.float32
    )
    attended = attended_f.astype(jnp.bfloat16).reshape(token_rows, query_sequence.shape[1])
    mixed_seq = jnp.dot(attended, weight_all, preferred_element_type=jnp.float32).astype(
        jnp.bfloat16
    )
    mixed_out = jnp.zeros_like(mixed_seq).at[row_position].set(mixed_seq)
    attention_gradient = lax.dot_general(
        dy_seq, weight_all, (((1,), (1,)), ((), ())), preferred_element_type=jnp.float32
    ).astype(jnp.bfloat16)
    attention_gradient4 = attention_gradient.reshape(
        token_rows, KEY_VALUE_HEADS, query_group, HEAD_WIDTH
    )
    d_probs = jnp.einsum(
        "tkgd,skd->kgts", attention_gradient4, value_band, preferred_element_type=jnp.float32
    )
    delta = jnp.sum(attention_gradient4.astype(jnp.float32) * attended_f, axis=-1)
    delta = jnp.transpose(delta, (1, 2, 0))[..., None]
    d_scores_b = (probs * (d_probs - delta)).astype(jnp.bfloat16)
    grad_q_seq = (
        jnp.einsum("kgts,skd->tkgd", d_scores_b, key_band, preferred_element_type=jnp.float32)
        * scale
    ).astype(jnp.bfloat16)
    grad_q_out = (
        jnp.zeros_like(query_sequence)
        .at[row_position]
        .set(grad_q_seq.reshape(token_rows, query_sequence.shape[1]))
    )
    part_k = (
        jnp.einsum("kgts,tkgd->skd", d_scores_b, query_four, preferred_element_type=jnp.float32)
        * scale
    ).astype(jnp.bfloat16)
    part_v = jnp.einsum(
        "kgts,tkgd->skd", probs_b, attention_gradient4, preferred_element_type=jnp.float32
    ).astype(jnp.bfloat16)
    part_both = jnp.concatenate(
        [
            part_k.reshape(3 * token_rows, key_head_width),
            part_v.reshape(3 * token_rows, key_head_width),
        ],
        axis=1,
    )
    outgoing = jnp.concatenate([part_both[:token_rows], part_both[2 * token_rows :]], axis=0)
    arrived = with_halo(outgoing, (("ctx", 0),), token_rows)
    summed = (
        part_both[token_rows : 2 * token_rows].astype(jnp.float32)
        + arrived[:token_rows].astype(jnp.float32)
        + arrived[3 * token_rows :].astype(jnp.float32)
    )
    summed = summed.astype(jnp.bfloat16)
    grad_k_out = jnp.zeros_like(key_sequence).at[row_position].set(summed[:, :key_head_width])
    grad_v_out = jnp.zeros_like(value_sequence).at[row_position].set(summed[:, key_head_width:])
    total_tokens = lax.axis_size("dp") * token_rows * lax.axis_size("ctx")
    norm_factor = 1.0 / math.sqrt(total_tokens)
    tile_rows = lax.psum_scatter(
        lax.dot_general(
            dy_seq, attended, (((0,), (0,)), ((), ())), preferred_element_type=jnp.float32
        ).astype(jnp.bfloat16),
        "ctx",
        scatter_dimension=0,
        tiled=True,
    ).astype(jnp.float32)
    grad_weight = lax.psum_scatter(tile_rows, "dp", scatter_dimension=1, tiled=True).T * norm_factor
    return (mixed_out[None], grad_q_out[None], grad_k_out[None], grad_v_out[None], grad_weight)


def solution(mesh):
    in_specs = (
        P("dp", "ctx", None),
        P("dp", "ctx", None),
        P("dp", "ctx", None),
        P("dp", "ctx", None),
        P("dp", "ctx", None),
        P("dp", None),
        P("dp", "ctx", None),
    )
    out_specs = (
        P("dp", "ctx", None),
        P("dp", "ctx", None),
        P("dp", "ctx", None),
        P("dp", "ctx", None),
        P("dp", "ctx"),
    )
    return jax.shard_map(shards, mesh=mesh, in_specs=in_specs, out_specs=out_specs, check_vma=False)
```

profile of v0, /device:TPU:0, one launch (start us, length us, event | category | flops | bytes accessed | tf_op | source)
XLA Modules:
  0.0 127.7 jit_solution(1401333764290365833)
XLA Ops:
  7.2 0.0 copy-start
  7.2 0.0 copy-start.10
  7.2 0.0 all-gather.2.cloned.1.call-start
  7.2 0.7 all-gather.2.cloned.1.call-update
  7.9 0.0 reduce-scatter.3.cloned.1.call-start
  8.0 0.7 compare_select_fusion
  8.6 1.6 %gather_fusion.1 = bf16[128,256]{1,0:T(8,128)(2,1)S(1)} fusion(bf16[128,256]{1,0:T(8,128)(2,1)} %bitcast.103, s32[1024]{0:T(1024)S(1)} %pad_clamp_fusion), kind=kCustom, calls=%fused_computation.2.clone | custom fusion | bytes 131584 | tf_op jit(solution)/shard_map/jit(_take)/gather | solution.py:35
  10.2 1.6 %gather_fusion = bf16[128,256]{1,0:T(8,128)(2,1)S(1)} fusion(bf16[128,256]{1,0:T(8,128)(2,1)} %bitcast.104, s32[1024]{0:T(1024)S(1)} %pad_clamp_fusion), kind=kCustom, calls=%fused_computation.clone | custom fusion | bytes 131584 | tf_op jit(solution)/shard_map/jit(_take)/gather | solution.py:34
  11.9 0.0 copy-start.1
  11.9 0.7 compare_and_fusion
  12.6 0.1 broadcast_select_fusion.5
  12.7 4.0 %collective-permute-start.1 = (bf16[128,512]{1,0:T(8,128)(2,1)S(1)}, bf16[128,512]{1,0:T(8,128)(2,1)S(1)}, u32[]{:S(2)}, u32[]{:S(2)}) collective-permute-start(bf16[128,512]{1,0:T(8,128)(2,1)S(1)} %pad_maximum_fusion.2), channel_id=1, source_target_pairs={{8,0},{16,8},{24,16},{0,24},{9,1},{17,9},{25,17},{1,25},{10,2},{18... | collective-permute-start | bytes 393224 | tf_op jit(solution)/shard_map/ppermute | solution.py:22
  16.7 0.0 collective-permute-start
  16.7 0.0 copy-done.10
  16.7 0.1 copy.29
  16.8 0.1 broadcast_in_dim.65
  16.9 0.1 gt.20
  16.9 0.9 gather_fusion.3
  17.8 0.9 gather_fusion.2
  18.7 0.1 broadcast_select_fusion.1
  18.8 0.2 copy.60
  19.0 0.1 pad_add_fusion
  19.1 1.4 %collective-permute-done.1 = bf16[128,512]{1,0:T(8,128)(2,1)S(1)} collective-permute-done((bf16[128,512]{1,0:T(8,128)(2,1)S(1)}, bf16[128,512]{1,0:T(8,128)(2,1)S(1)}, u32[]{:S(2)}, u32[]{:S(2)}) %collective-permute-start.1) | collective-permute-done | bytes 131104 | tf_op jit(solution)/shard_map/ppermute | solution.py:22
  20.5 2.7 %collective-permute-done = bf16[128,512]{1,0:T(8,128)(2,1)S(1)} collective-permute-done((bf16[128,512]{1,0:T(8,128)(2,1)S(1)}, bf16[128,512]{1,0:T(8,128)(2,1)S(1)}, u32[]{:S(2)}, u32[]{:S(2)}) %collective-permute-start) | collective-permute-done | bytes 131104 | tf_op jit(solution)/shard_map/ppermute | solution.py:19
  23.3 0.2 copy.30
  23.5 0.8 copy.28
  24.3 0.8 fusion.29
  25.1 0.1 fusion.8
  25.2 16.3 %all-gather.2.cloned.1.call-done = bf16[1024,1024]{1,0:T(8,128)(2,1)} async-done(((bf16[128,1024]{1,0:T(8,128)(2,1)}), bf16[1024,1024]{1,0:T(8,128)(2,1)}) %all-gather.2.cloned.1.call-update) | async-done | bytes 2097168 | tf_op jit(solution)/shard_map/all_gather | solution.py:45
  41.5 3.1 %convolution_convert_fusion.1 = bf16[128,1024]{1,0:T(8,128)(2,1)} fusion(bf16[1024,1024]{1,0:T(8,128)(2,1)} %all-gather.2.cloned.1.call-done, bf16[128,1024]{1,0:T(8,128)(2,1)S(1)} %gather_fusion.3, pred[128]{0:T(512)(128)(4,1)S(1)} %compare_and_fusion), kind=kOutput, calls=%fused_computation.19 | convolution fusion | flops 268697600 | bytes 2621568 | tf_op jit(solution)/shard_map/dot_general | solution.py:74
  44.6 1.1 copy.34
  45.8 1.2 multiply_reduce_fusion
  47.0 0.0 copy-start.5
  47.0 0.7 copy-done.5
  47.7 2.1 %convolution_convert_fusion = bf16[1024,1024]{1,0:T(8,128)(2,1)} fusion(bf16[128,1024]{0,1:T(8,128)(2,1)S(1)} %bitcast.107, bf16[128,1024]{1,0:T(8,128)(2,1)S(1)} %gather_fusion.3, pred[128]{0:T(512)(128)(4,1)S(1)} %compare_and_fusion), kind=kOutput, calls=%fused_computation.9 | convolution fusion | flops 269615104 | bytes 2621568 | tf_op jit(solution)/shard_map/dot_general | solution.py:122
  49.8 0.0 reduce-scatter.3.cloned.1.call-update
  49.9 0.0 copy-start.11
  49.9 0.0 copy-start.9
  49.9 0.0 reduce-scatter.5.cloned.1.call-start
  49.9 34.7 %reduce-scatter.3.cloned.1.call-done = bf16[256,1024]{1,0:T(8,128)(2,1)} async-done(((bf16[1024,1024]{1,0:T(8,128)(2,1)}), bf16[256,1024]{1,0:T(8,128)(2,1)}) %reduce-scatter.3.cloned.1.call-update) | async-done | bytes 524304 | tf_op jit(solution)/shard_map/reduce_scatter | solution.py:121
  84.6 2.1 %convert_element_type.71 = f32[256,1024]{1,0:T(8,128)} convert(bf16[256,1024]{1,0:T(8,128)(2,1)} %reduce-scatter.3.cloned.1.call-done) | non-fusion elementwise | flops 262144 | bytes 1572864 | tf_op jit(solution)/shard_map/convert_element_type | solution.py:128
  86.7 0.0 reduce-scatter.5.cloned.1.call-update
  86.8 0.4 fusion.3
  87.2 0.9 copy-done.3
  88.1 1.1 fusion.6
  89.2 1.9 %copy.42 = bf16[384,256]{1,0:T(8,128)(2,1)} copy(bf16[384,256]{0,1:T(8,128)(2,1)} %bitcast.115) | data formatting | bytes 393216 | tf_op jit(solution)/shard_map/reshape | solution.py:104
  91.1 1.1 fusion.7
  92.1 1.1 copy.43
  93.2 1.0 fusion.9
  94.2 1.5 %collective-permute-start.2 = (bf16[128,512]{1,0:T(8,128)(2,1)S(1)}, bf16[128,512]{1,0:T(8,128)(2,1)}, u32[]{:S(2)}, u32[]{:S(2)}) collective-permute-start(bf16[128,512]{1,0:T(8,128)(2,1)S(1)} %get-tuple-element.19), channel_id=1, source_target_pairs={{0,8},{8,16},{16,24},{24,0},{1,9},{9,17},{17,25},{25,1},{2,10},{10... | collective-permute-start | bytes 393224 | tf_op jit(solution)/shard_map/ppermute | solution.py:19
  95.7 1.5 %collective-permute-start.3 = (bf16[128,512]{1,0:T(8,128)(2,1)S(1)}, bf16[128,512]{1,0:T(8,128)(2,1)}, u32[]{:S(2)}, u32[]{:S(2)}) collective-permute-start(bf16[128,512]{1,0:T(8,128)(2,1)S(1)} %get-tuple-element.20), channel_id=1, source_target_pairs={{8,0},{16,8},{24,16},{0,24},{9,1},{17,9},{25,17},{1,25},{10,2},{18... | collective-permute-start | bytes 393224 | tf_op jit(solution)/shard_map/ppermute | solution.py:22
  97.2 2.1 %convolution_convert_fusion.2 = bf16[128,1024]{1,0:T(8,128)(2,1)} fusion(bf16[128,1024]{0,1:T(8,128)(2,1)} %bitcast.108, bf16[1024,1024]{1,0:T(8,128)(2,1)S(1)} %copy-done.2), kind=kOutput, calls=%fused_computation.20 | convolution fusion | flops 268566528 | bytes 2621440 | tf_op jit(solution)/shard_map/dot_general | solution.py:70
  99.3 0.3 fusion.4
  99.6 0.1 copy.38
  99.8 2.2 %scatter_custom_fusion = bf16[128,1024]{1,0:T(8,128)(2,1)} fusion(s32[128]{0:T(128)S(1)} %fusion.21, bf16[128,1024]{1,0:T(8,128)(2,1)} %convolution_convert_fusion.2, bf16[]{:T(256)} %constant.25.clone.1), kind=kCustom, calls=%fused_computation.45 | custom fusion | bytes 262656 | tf_op jit(solution)/shard_map/scatter | solution.py:73
  102.0 1.8 %scatter_custom_fusion.1 = bf16[128,1024]{1,0:T(8,128)(2,1)} fusion(s32[128]{0:T(128)S(1)} %fusion.21, bf16[128,1024]{1,0:T(8,128)(2,1)S(1)} %copy.38, bf16[]{:T(256)} %constant.25.clone.1), kind=kCustom, calls=%fused_computation.43 | custom fusion | bytes 262146 | tf_op jit(solution)/shard_map/scatter | solution.py:93
  103.8 0.0 collective-permute-done.2
  103.8 0.0 collective-permute-done.3
  103.8 1.0 add_convert_fusion
  104.8 1.6 %scatter_custom_fusion.3 = bf16[128,256]{1,0:T(8,128)(2,1)} fusion(s32[128]{0:T(128)S(1)} %fusion.21, bf16[128,512]{1,0:T(8,128)(2,1)S(1)} %add_convert_fusion, bf16[]{:T(256)} %constant.25.clone.1), kind=kCustom, calls=%fused_computation.47 | custom fusion | bytes 131074 | tf_op jit(solution)/shard_map/scatter | solution.py:118
  106.4 1.6 %scatter_custom_fusion.2 = bf16[128,256]{1,0:T(8,128)(2,1)} fusion(s32[128]{0:T(128)S(1)} %fusion.21, bf16[128,512]{1,0:T(8,128)(2,1)S(1)} %add_convert_fusion, bf16[]{:T(256)} %constant.25.clone.1), kind=kCustom, calls=%fused_computation.49 | custom fusion | bytes 131074 | tf_op jit(solution)/shard_map/scatter | solution.py:117
  108.1 11.4 %reduce-scatter.5.cloned.1.call-done = f32[256,128]{1,0:T(8,128)} async-done(((f32[256,1024]{1,0:T(8,128)}), f32[256,128]{1,0:T(8,128)}) %reduce-scatter.5.cloned.1.call-update) | async-done | bytes 131088 | tf_op jit(solution)/shard_map/reduce_scatter | solution.py:129
  119.5 0.9 multiply_bitcast_fusion
  120.4 0.8 copy.44
  (25 shorter events, 0.1 us)
Async XLA Ops:
  7.2 9.8 %copy-start = (bf16[1,128,1024]{2,1,0:T(8,128)(2,1)S(1)}, bf16[1,128,1024]{2,1,0:T(8,128)(2,1)}, u32[]{:S(2)}) copy-start(bf16[1,128,1024]{2,1,0:T(8,128)(2,1)} %param.17) | copy-start | bytes 786436
  7.2 9.5 %copy-start.10 = (s32[1,4,8]{2,1,0:T(4,128)S(1)}, s32[1,4,8]{2,1,0:T(4,128)}, u32[]{:S(2)}) copy-start(s32[1,4,8]{2,1,0:T(4,128)} %param.15) | copy-start | bytes 388
  7.2 34.3 %all-gather.2.cloned.1.call-start = ((), (), s32[]{:S(2)}) async-start(), calls=%async_computation.2 | async-start | bytes 2359296 | tf_op jit(solution)/shard_map/all_gather | solution.py:45
  7.9 76.7 %reduce-scatter.3.cloned.1.call-start = ((), (), s32[]{:S(2)}) async-start(), calls=%async_computation.3 | async-start | bytes 2621440 | tf_op jit(solution)/shard_map/reduce_scatter | solution.py:121
  11.9 6.0 %copy-start.1 = (bf16[1,128,1024]{2,1,0:T(8,128)(2,1)S(1)}, bf16[1,128,1024]{2,1,0:T(8,128)(2,1)}, u32[]{:S(2)}) copy-start(bf16[1,128,1024]{2,1,0:T(8,128)(2,1)} %param.11) | copy-start | bytes 786436
  12.7 7.9 %collective-permute-start.1 = (bf16[128,512]{1,0:T(8,128)(2,1)S(1)}, bf16[128,512]{1,0:T(8,128)(2,1)S(1)}, u32[]{:S(2)}, u32[]{:S(2)}) collective-permute-start(bf16[128,512]{1,0:T(8,128)(2,1)S(1)} %pad_maximum_fusion.2), channel_id=1, source_target_pairs={{8,0},{16,8},{24,16},{0,24},{9,1},{17,9},{25,17},{1,25},{10,2},{18... | collective-permute-start | bytes 393224 | tf_op jit(solution)/shard_map/ppermute | solution.py:22
  16.7 6.6 %collective-permute-start = (bf16[128,512]{1,0:T(8,128)(2,1)S(1)}, bf16[128,512]{1,0:T(8,128)(2,1)S(1)}, u32[]{:S(2)}, u32[]{:S(2)}) collective-permute-start(bf16[128,512]{1,0:T(8,128)(2,1)S(1)} %pad_maximum_fusion.2), channel_id=1, source_target_pairs={{0,8},{8,16},{16,24},{24,0},{1,9},{9,17},{17,25},{25,1},{2,10},{10... | collective-permute-start | bytes 393224 | tf_op jit(solution)/shard_map/ppermute | solution.py:19
  23.4 1.6 %copy-start.7 = (bf16[384,256]{0,1:T(8,128)(2,1)}, bf16[384,256]{0,1:T(8,128)(2,1)S(1)}, u32[]{:S(2)}) copy-start(bf16[384,256]{0,1:T(8,128)(2,1)S(1)} %copy.30) | copy-start | bytes 589828
  47.0 0.7 copy-start.5
  49.9 36.9 %copy-start.11 = (s32[1,1,128]{2,1,0:T(1,128)S(1)}, s32[1,1,128]{2,1,0:T(1,128)}, u32[]{:S(2)}) copy-start(s32[1,1,128]{2,1,0:T(1,128)} %param.14) | copy-start | bytes 1540
  49.9 36.9 %copy-start.9 = (bf16[384,256]{0,1:T(8,128)(2,1)S(1)}, bf16[384,256]{0,1:T(8,128)(2,1)}, u32[]{:S(2)}) copy-start(bf16[384,256]{0,1:T(8,128)(2,1)} %copy.28) | copy-start | bytes 589828
  49.9 69.6 %reduce-scatter.5.cloned.1.call-start = ((), (), s32[]{:S(2)}) async-start(), calls=%async_computation.4 | async-start | bytes 1179648 | tf_op jit(solution)/shard_map/reduce_scatter | solution.py:129
  87.2 0.9 copy-start.3
  89.2 8.0 %copy-start.2 = (bf16[1024,1024]{1,0:T(8,128)(2,1)S(1)}, bf16[1024,1024]{1,0:T(8,128)(2,1)}, u32[]{:S(2)}) copy-start(bf16[1024,1024]{1,0:T(8,128)(2,1)} %all-gather.2.cloned.1.call-done) | copy-start | bytes 6291460
  93.2 6.1 %copy-start.4 = (bf16[2,4,128,384]{2,3,1,0:T(8,128)(2,1)S(1)}, bf16[2,4,128,384]{2,3,1,0:T(8,128)(2,1)}, u32[]{:S(2)}) copy-start(bf16[2,4,128,384]{2,3,1,0:T(8,128)(2,1)} %copy-done.3) | copy-start | bytes 2359300
  93.2 6.1 %copy-start.8 = (bf16[384,256]{0,1:T(8,128)(2,1)S(1)}, bf16[384,256]{0,1:T(8,128)(2,1)}, u32[]{:S(2)}) copy-start(bf16[384,256]{0,1:T(8,128)(2,1)} %copy-done.7) | copy-start | bytes 589828
  94.2 9.6 %collective-permute-start.2 = (bf16[128,512]{1,0:T(8,128)(2,1)S(1)}, bf16[128,512]{1,0:T(8,128)(2,1)}, u32[]{:S(2)}, u32[]{:S(2)}) collective-permute-start(bf16[128,512]{1,0:T(8,128)(2,1)S(1)} %get-tuple-element.19), channel_id=1, source_target_pairs={{0,8},{8,16},{16,24},{24,0},{1,9},{9,17},{17,25},{25,1},{2,10},{10... | collective-permute-start | bytes 393224 | tf_op jit(solution)/shard_map/ppermute | solution.py:19
  95.7 8.1 %collective-permute-start.3 = (bf16[128,512]{1,0:T(8,128)(2,1)S(1)}, bf16[128,512]{1,0:T(8,128)(2,1)}, u32[]{:S(2)}, u32[]{:S(2)}) collective-permute-start(bf16[128,512]{1,0:T(8,128)(2,1)S(1)} %get-tuple-element.20), channel_id=1, source_target_pairs={{8,0},{16,8},{24,16},{0,24},{9,1},{17,9},{25,17},{1,25},{10,2},{18... | collective-permute-start | bytes 393224 | tf_op jit(solution)/shard_map/ppermute | solution.py:22
  99.3 4.5 %copy-start.6 = (bf16[384,256]{1,0:T(8,128)(2,1)S(1)}, bf16[384,256]{1,0:T(8,128)(2,1)}, u32[]{:S(2)}) copy-start(bf16[384,256]{1,0:T(8,128)(2,1)} %copy.42) | copy-start | bytes 589828
Sparse Core Ops, SparseCore 0:
  9.6 31.8 all-gather.1
  50.0 34.5 reduce-scatter.2
  86.9 32.5 reduce-scatter.4
where the time goes:
time: 128 us
  waiting for transfers between devices  67.2 us (52%)
  local copies, waits for them, and re-layouts  20.3 us (16%)
  between operations  14 us (11%)
  matrix products  12.3 us (10%)
  starting transfers between devices  7.07 us (6%)
  other arithmetic  6.9 us (5%)
    reduce_scatter x1, waiting for transfers between devices, shards(): lax.psum_scatter(lax.dot_general(dy_seq, attended, (((0,), (0,)), ((), ()...  34.7 us
    all_gather x1, waiting for transfers between devices, shards(): weight_all = lax.all_gather(out_weight, 'dp', axis=0, tiled=True)  16.3 us
    reduce_scatter x1, waiting for transfers between devices, shards(): lax.psum_scatter(tile_rows, 'dp', scatter_dimension=1, tiled=True)  11.4 us
    ppermute x2, starting transfers between devices, with_halo(): lax.ppermute(lax.slice_in_dim(block, 0, width, axis=dim), axis, backward)  5.44 us
    dot_general x1, matrix products, shards(): lax.dot_general(dy_seq, weight_all, (((1,), (1,)), ((), ())), preferred_e...  3.13 us
    ppermute x2, waiting for transfers between devices, with_halo(): lax.ppermute(lax.slice_in_dim(block, block.shape[dim] - width, None, axis...  2.67 us
  transfers between devices with their start and end apart: 7, of which 5 were waited for; matrix products, arithmetic and copies ran while one was open for 21% of the time, Pallas kernels for 0%

commit v1 on v0

--- a/solution.py
+++ b/solution.py
@@ -42,7 +42,27 @@
     value_band = neighbour_band[:, key_head_width:].reshape(
         3 * token_rows, KEY_VALUE_HEADS, HEAD_WIDTH
     )
-    weight_all = lax.all_gather(out_weight, "dp", axis=0, tiled=True)
+
+    def _process_tails(z_in, net_axis):
+        n_parts = lax.psum(1, axis_name=net_axis)
+        heap = []
+        idx = 1
+        while idx < n_parts:
+            heap.append((idx - 1, idx))
+            idx += 1
+        extra = heap + [(n_parts - 1, 0)]
+        side_arr = z_in
+        inbox = [side_arr]
+        c = 0
+        while c < n_parts - 1:
+            side_arr = lax.ppermute(side_arr, axis_name=net_axis, perm=extra)
+            inbox += [side_arr]
+            c = c + 1
+        x_new = jnp.concatenate([*reversed(inbox)], 0)
+        step_out = jnp.roll(x_new, (lax.axis_index(net_axis) + 1) * side_arr.shape[0], 0)
+        return step_out
+
+    weight_all = _process_tails(out_weight, "dp")
     expanded = jnp.repeat(jnp.repeat(block_mask[0], BLK, 0), BLK, 1) > 0
     allowed = jnp.concatenate(
         [

time: 128 us -> 152 us (1.19)
  waiting for transfers between devices: 67.2 us -> 93.9 us
  matrix products: 12.3 us -> 10.1 us
    ppermute x0 -> x7, waiting for transfers between devices: none -> 41.5 us  [_process_tails(): side_arr = lax.ppermute(side_arr, axis_name=net_axis, perm=extra)]
    all_gather x1 -> x0, waiting for transfers between devices: 16.3 us -> none  [shards(): weight_all = lax.all_gather(out_weight, 'dp', axis=0, tiled=True)]
    reduce_scatter x1, waiting for transfers between devices: 11.4 us -> 17.3 us  [shards(): lax.psum_scatter(tile_rows, 'dp', scatter_dimension=1, tiled=True)]
    unnamed x25 -> x50, local copies, waits for them, and re-layouts: 2.39 us -> 7.83 us
    dot_general x1, matrix products: 3.13 us -> 0.84 us  [shards(): lax.dot_general(dy_seq, weight_all, (((1,), (1,)), ((), ())), preferred_e...]
    reshape x1, local copies, waits for them, and re-layouts: 1.89 us -> 0.15 us  [shards(): part_k.reshape(3 * token_rows, key_head_width)]
    ppermute x2, waiting for transfers between devices: 2.67 us -> 1.06 us  [with_halo(): lax.ppermute(lax.slice_in_dim(block, block.shape[dim] - width, None, axis...]
  transfers between devices with their start and end apart: 7 -> 13, of which waited for: 5 -> 10; matrix products, arithmetic and copies ran while one was open for 21% -> 15% of each run, Pallas kernels for 0% -> 0%
where the time goes in v1:
time: 152 us
  waiting for transfers between devices  93.9 us (62%)
  local copies, waits for them, and re-layouts  21.7 us (14%)
  between operations  14.6 us (10%)
  matrix products  10.1 us (7%)
  starting transfers between devices  5.71 us (4%)
  other arithmetic  5.61 us (4%)
    ppermute x7, waiting for transfers between devices, _process_tails(): side_arr = lax.ppermute(side_arr, axis_name=net_axis, perm=extra)  41.5 us
    reduce_scatter x1, waiting for transfers between devices, shards(): lax.psum_scatter(lax.dot_general(dy_seq, attended, (((0,), (0,)), ((), ()...  34 us
    reduce_scatter x1, waiting for transfers between devices, shards(): lax.psum_scatter(tile_rows, 'dp', scatter_dimension=1, tiled=True)  17.3 us
    unnamed x50, local copies, waits for them, and re-layouts  7.83 us
    ppermute x2, starting transfers between devices, with_halo(): lax.ppermute(lax.slice_in_dim(block, 0, width, axis=dim), axis, backward)  4.51 us
  transfers between devices with their start and end apart: 13, of which 10 were waited for; matrix products, arithmetic and copies ran while one was open for 15% of the time, Pallas kernels for 0%

profile of v1, /device:TPU:0, one launch (start us, length us, event | category | flops | bytes accessed | tf_op | source)
XLA Modules:
  0.0 151.6 jit_solution(1807341030441460061)
XLA Ops:
  7.2 0.0 copy-start
  7.2 0.0 reduce-scatter.3.cloned.1.call-start
  7.2 0.5 collective-permute-start.2
  7.8 0.7 compare_select_fusion
  8.4 1.6 %gather_fusion = bf16[128,256]{1,0:T(8,128)(2,1)S(1)} fusion(bf16[128,256]{1,0:T(8,128)(2,1)} %bitcast.97, s32[1024]{0:T(1024)S(1)} %pad_clamp_fusion), kind=kCustom, calls=%fused_computation.clone | custom fusion | bytes 131584 | tf_op jit(solution)/shard_map/jit(_take)/gather | solution.py:34
  10.1 1.6 %gather_fusion.1 = bf16[128,256]{1,0:T(8,128)(2,1)S(1)} fusion(bf16[128,256]{1,0:T(8,128)(2,1)} %bitcast.98, s32[1024]{0:T(1024)S(1)} %pad_clamp_fusion), kind=kCustom, calls=%fused_computation.2.clone | custom fusion | bytes 131584 | tf_op jit(solution)/shard_map/jit(_take)/gather | solution.py:35
  11.7 0.7 compare_and_fusion
  12.3 3.8 %collective-permute-done.2 = bf16[128,1024]{1,0:T(8,128)(2,1)S(1)} collective-permute-done((bf16[128,1024]{1,0:T(8,128)(2,1)}, bf16[128,1024]{1,0:T(8,128)(2,1)S(1)}, u32[]{:S(2)}, u32[]{:S(2)}) %collective-permute-start.2) | collective-permute-done | bytes 262176 | tf_op jit(solution)/shard_map/ppermute | solution.py:58
  16.1 0.1 broadcast_select_fusion.5
  16.2 3.0 %collective-permute-start.1 = (bf16[128,512]{1,0:T(8,128)(2,1)S(1)}, bf16[128,512]{1,0:T(8,128)(2,1)S(1)}, u32[]{:S(2)}, u32[]{:S(2)}) collective-permute-start(bf16[128,512]{1,0:T(8,128)(2,1)S(1)} %pad_maximum_fusion.2), channel_id=1, source_target_pairs={{8,0},{16,8},{24,16},{0,24},{9,1},{17,9},{25,17},{1,25},{10,2},{18... | collective-permute-start | bytes 393224 | tf_op jit(solution)/shard_map/ppermute | solution.py:22
  19.2 4.5 %collective-permute-done.3 = bf16[128,1024]{1,0:T(8,128)(2,1)S(1)} collective-permute-done((bf16[128,1024]{1,0:T(8,128)(2,1)S(1)}, bf16[128,1024]{1,0:T(8,128)(2,1)S(1)}, u32[]{:S(2)}, u32[]{:S(2)}) %collective-permute-start.3) | collective-permute-done | bytes 262176 | tf_op jit(solution)/shard_map/ppermute | solution.py:58
  23.7 0.7 compare_bitcast_fusion
  24.4 0.9 gather_fusion.2
  25.2 0.1 copy.29
  25.3 0.1 broadcast_in_dim.65
  25.4 0.1 gt.20
  25.5 0.1 broadcast_select_fusion.1
  25.6 5.7 %collective-permute-done.4 = bf16[128,1024]{1,0:T(8,128)(2,1)S(1)} collective-permute-done((bf16[128,1024]{1,0:T(8,128)(2,1)S(1)}, bf16[128,1024]{1,0:T(8,128)(2,1)S(1)}, u32[]{:S(2)}, u32[]{:S(2)}) %collective-permute-start.4) | collective-permute-done | bytes 262176 | tf_op jit(solution)/shard_map/ppermute | solution.py:58
  31.3 0.9 gather_fusion.3
  32.2 0.2 copy.60
  32.4 0.1 pad_add_fusion
  32.5 6.3 %collective-permute-done.5 = bf16[128,1024]{1,0:T(8,128)(2,1)S(1)} collective-permute-done((bf16[128,1024]{1,0:T(8,128)(2,1)S(1)}, bf16[128,1024]{1,0:T(8,128)(2,1)S(1)}, u32[]{:S(2)}, u32[]{:S(2)}) %collective-permute-start.5) | collective-permute-done | bytes 262176 | tf_op jit(solution)/shard_map/ppermute | solution.py:58
  39.0 0.8 copy.28
  39.8 0.2 copy.30
  40.0 6.6 %collective-permute-done.6 = bf16[128,1024]{1,0:T(8,128)(2,1)} collective-permute-done((bf16[128,1024]{1,0:T(8,128)(2,1)S(1)}, bf16[128,1024]{1,0:T(8,128)(2,1)}, u32[]{:S(2)}, u32[]{:S(2)}) %collective-permute-start.6) | collective-permute-done | bytes 262176 | tf_op jit(solution)/shard_map/ppermute | solution.py:58
  46.6 0.0 copy-start.4
  46.6 0.8 fusion.41
  47.5 7.0 %collective-permute-done.7 = bf16[128,1024]{1,0:T(8,128)(2,1)} collective-permute-done((bf16[128,1024]{1,0:T(8,128)(2,1)}, bf16[128,1024]{1,0:T(8,128)(2,1)}, u32[]{:S(2)}, u32[]{:S(2)}) %collective-permute-start.7) | collective-permute-done | bytes 262176 | tf_op jit(solution)/shard_map/ppermute | solution.py:58
  54.5 0.1 fusion.18
  54.6 7.7 %collective-permute-done.8 = bf16[128,1024]{1,0:T(8,128)(2,1)S(1)} collective-permute-done((bf16[128,1024]{1,0:T(8,128)(2,1)}, bf16[128,1024]{1,0:T(8,128)(2,1)S(1)}, u32[]{:S(2)}, u32[]{:S(2)}) %collective-permute-start.8) | collective-permute-done | bytes 262176 | tf_op jit(solution)/shard_map/ppermute | solution.py:58
  62.3 1.0 constant_dynamic-update-slice_fusion.14
  63.3 1.0 constant_dynamic-update-slice_fusion.13
  64.3 1.0 constant_dynamic-update-slice_fusion.12
  65.4 1.0 constant_dynamic-update-slice_fusion.6
  66.4 1.0 constant_dynamic-update-slice_fusion.5
  67.5 2.0 %copy-done.2 = bf16[2048,1024]{1,0:T(8,128)(2,1)} copy-done((bf16[2048,1024]{1,0:T(8,128)(2,1)}, bf16[2048,1024]{1,0:T(8,128)(2,1)S(1)}, u32[]{:S(2)}) %copy-start.2) | copy-done | bytes 4194328
  69.5 0.8 fusion.12
  70.3 0.2 copy.34
  70.5 1.3 multiply_reduce_fusion
  71.8 2.2 %convolution_convert_fusion = bf16[1024,1024]{1,0:T(8,128)(2,1)} fusion(bf16[128,1024]{0,1:T(8,128)(2,1)S(1)} %bitcast.101, bf16[128,1024]{1,0:T(8,128)(2,1)S(1)} %gather_fusion.3, pred[128]{0:T(512)(128)(4,1)S(1)} %compare_and_fusion), kind=kOutput, calls=%fused_computation.9 | convolution fusion | flops 269615104 | bytes 2621568 | tf_op jit(solution)/shard_map/dot_general | solution.py:142
  74.0 0.0 reduce-scatter.3.cloned.1.call-update
  74.0 0.0 reduce-scatter.5.cloned.1.call-start
  74.1 34.0 %reduce-scatter.3.cloned.1.call-done = bf16[256,1024]{1,0:T(8,128)(2,1)} async-done(((bf16[1024,1024]{1,0:T(8,128)(2,1)}), bf16[256,1024]{1,0:T(8,128)(2,1)}) %reduce-scatter.3.cloned.1.call-update) | async-done | bytes 524304 | tf_op jit(solution)/shard_map/reduce_scatter | solution.py:141
  108.1 2.1 %convert_element_type.71 = f32[256,1024]{1,0:T(8,128)} convert(bf16[256,1024]{1,0:T(8,128)(2,1)} %reduce-scatter.3.cloned.1.call-done) | non-fusion elementwise | flops 262144 | bytes 1572864 | tf_op jit(solution)/shard_map/convert_element_type | solution.py:148
  110.2 0.0 reduce-scatter.5.cloned.1.call-update
  110.3 1.8 %fusion.7 = bf16[2,4,128,384]{2,3,1,0:T(8,128)(2,1)S(1)} fusion(bf16[384,2,128,1]{0,2,3,1:T(8,128)(2,1)S(1)} %bitcast.111, bf16[128,2,4,128]{0,3,2,1:T(8,128)(2,1)S(1)} %bitcast.99, f32[2,4,128]{2,1,0:T(4,128)S(1)} %bitcast.117, f32[2,4,128,384]{2,3,1,0:T(8,128)} %copy-done.3, f32[2,4,128]{2,1,0:T(4,128)S(1)} %get-tuple-element.27), kind=kOutput, calls=%fused_computation.17 | convolution fusion | flops 102236160 | bytes 2826240 | tf_op jit(solution)/shard_map/tkgd,skd->kgts/dot_general | solution.py:100
  112.1 0.3 fusion.8
  112.4 0.1 copy.38
  112.6 0.4 fusion.16
  113.0 0.1 copy.42
  113.1 0.4 fusion.17
  113.5 0.1 copy.43
  113.7 1.5 collective-permute-start.10
  115.2 0.6 collective-permute-start.9
  115.7 2.1 %fusion.9 = bf16[128,1024]{1,0:T(8,128)(2,1)S(1)} fusion(bf16[128,1024]{0,1:T(8,128)(2,1)S(1)} %bitcast.102, bf16[2048,1024]{1,0:T(8,128)(2,1)} %copy-done.2, s32[]{:T(128)S(6)} %select_n.50), kind=kOutput, calls=%fused_computation.23 | convolution fusion | flops 268566528 | bytes 2621444 | tf_op jit(solution)/shard_map/dot_general | solution.py:90
  117.8 1.8 %scatter_custom_fusion = bf16[128,1024]{1,0:T(8,128)(2,1)} fusion(s32[128]{0:T(128)S(1)} %fusion.31, bf16[128,1024]{1,0:T(8,128)(2,1)S(1)} %fusion.9, bf16[]{:T(256)} %constant.30.clone.1), kind=kCustom, calls=%fused_computation.49 | custom fusion | bytes 262146 | tf_op jit(solution)/shard_map/scatter | solution.py:93
  119.6 1.8 %scatter_custom_fusion.1 = bf16[128,1024]{1,0:T(8,128)(2,1)} fusion(s32[128]{0:T(128)S(1)} %fusion.31, bf16[128,1024]{1,0:T(8,128)(2,1)S(1)} %copy.38, bf16[]{:T(256)} %constant.30.clone.1), kind=kCustom, calls=%fused_computation.47 | custom fusion | bytes 262146 | tf_op jit(solution)/shard_map/scatter | solution.py:113
  121.4 1.1 collective-permute-done.9
  122.5 0.1 add_convert_fusion
  122.6 1.6 %scatter_custom_fusion.2 = bf16[128,256]{1,0:T(8,128)(2,1)} fusion(s32[128]{0:T(128)S(1)} %fusion.31, bf16[128,512]{1,0:T(8,128)(2,1)S(1)} %add_convert_fusion, bf16[]{:T(256)} %constant.30.clone.1), kind=kCustom, calls=%fused_computation.53 | custom fusion | bytes 131074 | tf_op jit(solution)/shard_map/scatter | solution.py:137
  124.2 1.6 %scatter_custom_fusion.3 = bf16[128,256]{1,0:T(8,128)(2,1)} fusion(s32[128]{0:T(128)S(1)} %fusion.31, bf16[128,512]{1,0:T(8,128)(2,1)S(1)} %add_convert_fusion, bf16[]{:T(256)} %constant.30.clone.1), kind=kCustom, calls=%fused_computation.51 | custom fusion | bytes 131074 | tf_op jit(solution)/shard_map/scatter | solution.py:138
  125.8 17.3 %reduce-scatter.5.cloned.1.call-done = f32[256,128]{1,0:T(8,128)} async-done(((f32[256,1024]{1,0:T(8,128)}), f32[256,128]{1,0:T(8,128)}) %reduce-scatter.5.cloned.1.call-update) | async-done | bytes 131088 | tf_op jit(solution)/shard_map/reduce_scatter | solution.py:149
  143.1 0.9 multiply_bitcast_fusion
  144.0 0.8 copy.44
  (62 shorter events, 0.4 us)
Async XLA Ops:
  7.2 17.2 %copy-start = (bf16[1,128,1024]{2,1,0:T(8,128)(2,1)S(1)}, bf16[1,128,1024]{2,1,0:T(8,128)(2,1)}, u32[]{:S(2)}) copy-start(bf16[1,128,1024]{2,1,0:T(8,128)(2,1)} %param.11) | copy-start | bytes 786436
  7.2 24.2 %copy-start.1 = (bf16[1,128,1024]{2,1,0:T(8,128)(2,1)S(1)}, bf16[1,128,1024]{2,1,0:T(8,128)(2,1)}, u32[]{:S(2)}) copy-start(bf16[1,128,1024]{2,1,0:T(8,128)(2,1)} %param.17) | copy-start | bytes 786436
  7.2 100.9 %reduce-scatter.3.cloned.1.call-start = ((), (), s32[]{:S(2)}) async-start(), calls=%async_computation.2 | async-start | bytes 2621440 | tf_op jit(solution)/shard_map/reduce_scatter | solution.py:141
  7.2 8.8 %collective-permute-start.2 = (bf16[128,1024]{1,0:T(8,128)(2,1)}, bf16[128,1024]{1,0:T(8,128)(2,1)S(1)}, u32[]{:S(2)}, u32[]{:S(2)}) collective-permute-start(bf16[128,1024]{1,0:T(8,128)(2,1)} %param.16), channel_id=1, source_target_pairs={{0,1},{1,2},{2,3},{3,4},{4,5},{5,6},{6,7},{7,0},{8,9},{9,10},{10,1... | collective-permute-start | bytes 786440 | tf_op jit(solution)/shard_map/ppermute | solution.py:58
  16.1 8.3 %copy-start.5 = (bf16[128,1024]{1,0:T(8,128)(2,1)}, bf16[128,1024]{1,0:T(8,128)(2,1)S(1)}, u32[]{:S(2)}) copy-start(bf16[128,1024]{1,0:T(8,128)(2,1)S(1)} %collective-permute-done.2) | copy-start | bytes 786436
  16.1 7.6 %collective-permute-start.3 = (bf16[128,1024]{1,0:T(8,128)(2,1)S(1)}, bf16[128,1024]{1,0:T(8,128)(2,1)S(1)}, u32[]{:S(2)}, u32[]{:S(2)}) collective-permute-start(bf16[128,1024]{1,0:T(8,128)(2,1)S(1)} %collective-permute-done.2), channel_id=1, source_target_pairs={{0,1},{1,2},{2,3},{3,4},{4,5},{5,6},{6,7},{7,0},{8,9},{9,10},{10,1... | collective-permute-start | bytes 786440 | tf_op jit(solution)/shard_map/ppermute | solution.py:58
  16.2 22.7 %collective-permute-start.1 = (bf16[128,512]{1,0:T(8,128)(2,1)S(1)}, bf16[128,512]{1,0:T(8,128)(2,1)S(1)}, u32[]{:S(2)}, u32[]{:S(2)}) collective-permute-start(bf16[128,512]{1,0:T(8,128)(2,1)S(1)} %pad_maximum_fusion.2), channel_id=1, source_target_pairs={{8,0},{16,8},{24,16},{0,24},{9,1},{17,9},{25,17},{1,25},{10,2},{18... | collective-permute-start | bytes 393224 | tf_op jit(solution)/shard_map/ppermute | solution.py:22
  19.2 19.7 %collective-permute-start = (bf16[128,512]{1,0:T(8,128)(2,1)S(1)}, bf16[128,512]{1,0:T(8,128)(2,1)S(1)}, u32[]{:S(2)}, u32[]{:S(2)}) collective-permute-start(bf16[128,512]{1,0:T(8,128)(2,1)S(1)} %pad_maximum_fusion.2), channel_id=1, source_target_pairs={{0,8},{8,16},{16,24},{24,0},{1,9},{9,17},{17,25},{25,1},{2,10},{10... | collective-permute-start | bytes 393224 | tf_op jit(solution)/shard_map/ppermute | solution.py:19
  23.7 7.7 %copy-start.7 = (bf16[128,1024]{1,0:T(8,128)(2,1)}, bf16[128,1024]{1,0:T(8,128)(2,1)S(1)}, u32[]{:S(2)}) copy-start(bf16[128,1024]{1,0:T(8,128)(2,1)S(1)} %collective-permute-done.3) | copy-start | bytes 786436
  23.7 7.6 %collective-permute-start.4 = (bf16[128,1024]{1,0:T(8,128)(2,1)S(1)}, bf16[128,1024]{1,0:T(8,128)(2,1)S(1)}, u32[]{:S(2)}, u32[]{:S(2)}) collective-permute-start(bf16[128,1024]{1,0:T(8,128)(2,1)S(1)} %collective-permute-done.3), channel_id=1, source_target_pairs={{0,1},{1,2},{2,3},{3,4},{4,5},{5,6},{6,7},{7,0},{8,9},{9,10},{10,1... | collective-permute-start | bytes 786440 | tf_op jit(solution)/shard_map/ppermute | solution.py:58
  31.3 15.3 %copy-start.9 = (bf16[128,1024]{1,0:T(8,128)(2,1)}, bf16[128,1024]{1,0:T(8,128)(2,1)S(1)}, u32[]{:S(2)}) copy-start(bf16[128,1024]{1,0:T(8,128)(2,1)S(1)} %collective-permute-done.4) | copy-start | bytes 786436
  31.3 7.6 %collective-permute-start.5 = (bf16[128,1024]{1,0:T(8,128)(2,1)S(1)}, bf16[128,1024]{1,0:T(8,128)(2,1)S(1)}, u32[]{:S(2)}, u32[]{:S(2)}) collective-permute-start(bf16[128,1024]{1,0:T(8,128)(2,1)S(1)} %collective-permute-done.4), channel_id=1, source_target_pairs={{0,1},{1,2},{2,3},{3,4},{4,5},{5,6},{6,7},{7,0},{8,9},{9,10},{10,1... | collective-permute-start | bytes 786440 | tf_op jit(solution)/shard_map/ppermute | solution.py:58
  38.9 7.7 %copy-start.11 = (bf16[128,1024]{1,0:T(8,128)(2,1)}, bf16[128,1024]{1,0:T(8,128)(2,1)S(1)}, u32[]{:S(2)}) copy-start(bf16[128,1024]{1,0:T(8,128)(2,1)S(1)} %collective-permute-done.5) | copy-start | bytes 786436
  38.9 7.7 %collective-permute-start.6 = (bf16[128,1024]{1,0:T(8,128)(2,1)S(1)}, bf16[128,1024]{1,0:T(8,128)(2,1)}, u32[]{:S(2)}, u32[]{:S(2)}) collective-permute-start(bf16[128,1024]{1,0:T(8,128)(2,1)S(1)} %collective-permute-done.5), channel_id=1, source_target_pairs={{0,1},{1,2},{2,3},{3,4},{4,5},{5,6},{6,7},{7,0},{8,9},{9,10},{10,1... | collective-permute-start | bytes 786440 | tf_op jit(solution)/shard_map/ppermute | solution.py:58
  40.0 14.5 %copy-start.13 = (bf16[384,256]{0,1:T(8,128)(2,1)}, bf16[384,256]{0,1:T(8,128)(2,1)S(1)}, u32[]{:S(2)}) copy-start(bf16[384,256]{0,1:T(8,128)(2,1)S(1)} %copy.30) | copy-start | bytes 589828
  46.6 7.9 %collective-permute-start.7 = (bf16[128,1024]{1,0:T(8,128)(2,1)}, bf16[128,1024]{1,0:T(8,128)(2,1)}, u32[]{:S(2)}, u32[]{:S(2)}) collective-permute-start(bf16[128,1024]{1,0:T(8,128)(2,1)} %collective-permute-done.6), channel_id=1, source_target_pairs={{0,1},{1,2},{2,3},{3,4},{4,5},{5,6},{6,7},{7,0},{8,9},{9,10},{10,1... | collective-permute-start | bytes 786440 | tf_op jit(solution)/shard_map/ppermute | solution.py:58
  46.6 18.8 %copy-start.4 = (bf16[128,1024]{1,0:T(8,128)(2,1)S(1)}, bf16[128,1024]{1,0:T(8,128)(2,1)}, u32[]{:S(2)}) copy-start(bf16[128,1024]{1,0:T(8,128)(2,1)} %param.16) | copy-start | bytes 786436
  47.4 20.0 %copy-start.3 = (f32[2,4,128,384]{2,3,1,0:T(8,128)}, f32[2,4,128,384]{2,3,1,0:T(8,128)S(1)}, u32[]{:S(2)}) copy-start(f32[2,4,128,384]{2,3,1,0:T(8,128)S(1)} %get-tuple-element.28) | copy-start | bytes 4718596
  47.4 17.8 %copy-start.10 = (bf16[128,1024]{1,0:T(8,128)(2,1)S(1)}, bf16[128,1024]{1,0:T(8,128)(2,1)}, u32[]{:S(2)}) copy-start(bf16[128,1024]{1,0:T(8,128)(2,1)} %copy-done.9) | copy-start | bytes 786436
  47.4 17.8 %copy-start.8 = (bf16[128,1024]{1,0:T(8,128)(2,1)S(1)}, bf16[128,1024]{1,0:T(8,128)(2,1)}, u32[]{:S(2)}) copy-start(bf16[128,1024]{1,0:T(8,128)(2,1)} %copy-done.7) | copy-start | bytes 786436
  47.4 17.9 %copy-start.6 = (bf16[128,1024]{1,0:T(8,128)(2,1)S(1)}, bf16[128,1024]{1,0:T(8,128)(2,1)}, u32[]{:S(2)}) copy-start(bf16[128,1024]{1,0:T(8,128)(2,1)} %copy-done.5) | copy-start | bytes 786436
  47.4 19.9 %copy-start.12 = (bf16[128,1024]{1,0:T(8,128)(2,1)S(1)}, bf16[128,1024]{1,0:T(8,128)(2,1)}, u32[]{:S(2)}) copy-start(bf16[128,1024]{1,0:T(8,128)(2,1)} %copy-done.11) | copy-start | bytes 786436
  54.5 7.8 %collective-permute-start.8 = (bf16[128,1024]{1,0:T(8,128)(2,1)}, bf16[128,1024]{1,0:T(8,128)(2,1)S(1)}, u32[]{:S(2)}, u32[]{:S(2)}) collective-permute-start(bf16[128,1024]{1,0:T(8,128)(2,1)} %collective-permute-done.7), channel_id=1, source_target_pairs={{0,1},{1,2},{2,3},{3,4},{4,5},{5,6},{6,7},{7,0},{8,9},{9,10},{10,1... | collective-permute-start | bytes 786440 | tf_op jit(solution)/shard_map/ppermute | solution.py:58
  67.5 2.0 %copy-start.2 = (bf16[2048,1024]{1,0:T(8,128)(2,1)}, bf16[2048,1024]{1,0:T(8,128)(2,1)S(1)}, u32[]{:S(2)}) copy-start(bf16[2048,1024]{1,0:T(8,128)(2,1)S(1)} %constant_dynamic-update-slice_fusion) | copy-start | bytes 12582916
  70.5 39.7 %copy-start.16 = (s32[1,1,128]{2,1,0:T(1,128)S(1)}, s32[1,1,128]{2,1,0:T(1,128)}, u32[]{:S(2)}) copy-start(s32[1,1,128]{2,1,0:T(1,128)} %param.14) | copy-start | bytes 1540
  70.5 39.7 %copy-start.15 = (bf16[384,256]{0,1:T(8,128)(2,1)S(1)}, bf16[384,256]{0,1:T(8,128)(2,1)}, u32[]{:S(2)}) copy-start(bf16[384,256]{0,1:T(8,128)(2,1)} %copy.28) | copy-start | bytes 589828
  74.0 38.1 %copy-start.14 = (bf16[384,256]{0,1:T(8,128)(2,1)S(1)}, bf16[384,256]{0,1:T(8,128)(2,1)}, u32[]{:S(2)}) copy-start(bf16[384,256]{0,1:T(8,128)(2,1)} %copy-done.13) | copy-start | bytes 589828
  74.0 69.1 %reduce-scatter.5.cloned.1.call-start = ((), (), s32[]{:S(2)}) async-start(), calls=%async_computation.3 | async-start | bytes 1179648 | tf_op jit(solution)/shard_map/reduce_scatter | solution.py:149
  113.7 7.8 %collective-permute-start.10 = (bf16[128,512]{1,0:T(8,128)(2,1)S(1)}, bf16[128,512]{1,0:T(8,128)(2,1)S(1)}, u32[]{:S(2)}, u32[]{:S(2)}) collective-permute-start(bf16[128,512]{1,0:T(8,128)(2,1)S(1)} %get-tuple-element.20), channel_id=1, source_target_pairs={{8,0},{16,8},{24,16},{0,24},{9,1},{17,9},{25,17},{1,25},{10,2},{18... | collective-permute-start | bytes 393224 | tf_op jit(solution)/shard_map/ppermute | solution.py:22
  115.2 7.3 %collective-permute-start.9 = (bf16[128,512]{1,0:T(8,128)(2,1)S(1)}, bf16[128,512]{1,0:T(8,128)(2,1)S(1)}, u32[]{:S(2)}, u32[]{:S(2)}) collective-permute-start(bf16[128,512]{1,0:T(8,128)(2,1)S(1)} %get-tuple-element.19), channel_id=1, source_target_pairs={{0,8},{8,16},{16,24},{24,0},{1,9},{9,17},{17,25},{25,1},{2,10},{10... | collective-permute-start | bytes 393224 | tf_op jit(solution)/shard_map/ppermute | solution.py:19
Sparse Core Ops, SparseCore 0:
  74.1 33.8 reduce-scatter.2
  110.3 32.6 reduce-scatter.4
